TPU v7x, 256 devices: a whole 4x4x8 slice. The times are simulated.
256 devices in a mesh: expert: 4 (over z_lo), etp: 16 (over y, x), tp: 4 (over z_hi, core).
Axes of the slice: x: 4, y: 4, z: 8 (z_hi: 2, z_lo: 4; z = z_hi * 4 + z_lo), core: 2. Of those that a mesh axis runs over, the one named last changes fastest.
Arguments:
- d_out: bfloat16 [2048, 6144], P(('expert', 'tp'), 'etp'), may hold values from -6 to 6
- expert_ids: int32 [2048, 2], P(('expert', 'tp')), may hold values from 0 to 3, all different within a row; in each aligned block of 128 rows (0 to 127, 128 to 255, ...) at most 64 rows name the same one
- gate_weights: float32 [2048, 2], P(('expert', 'tp')), may hold values from 0.05 to 0.95, as said below
- saved_gate: bfloat16 [4, 1024, 16384], P('expert', None, ('etp', 'tp')), may hold values from -8 to 8
- saved_up: bfloat16 [4, 1024, 16384], P('expert', None, ('etp', 'tp')), may hold values from -6 to 6
- w_gate: bfloat16 [4, 6144, 16384], P('expert', None, ('etp', 'tp')), may hold values from -0.078125 to 0.078125
- w_up: bfloat16 [4, 6144, 16384], P('expert', None, ('etp', 'tp')), may hold values from -0.078125 to 0.078125
- w_down: bfloat16 [4, 16384, 6144], P('expert', ('etp', 'tp')), may hold values from -0.046875 to 0.046875
- w_out: bfloat16 [6144, 6144], P('tp', 'etp'), may hold values from -0.078125 to 0.078125
Outputs:
- d_hidden: bfloat16 [2048, 6144], P(('expert', 'tp'), 'etp')
- d_heads: bfloat16 [2048, 6144], P(('expert', 'etp'), 'tp')
Inputs may be any that keep to these rules, and one draw needn't show every extreme that they name: `expert_ids`: each token names two different experts; in every block of 128 tokens every expert is named by exactly 64 tokens. `gate_weights`: a token's two weights sum to one.
All inputs are finite; a program needn't handle non-finite values.
Results may differ from a plain program's by a relative error of at most 0.02.
Values may be sent and summed in bfloat16 or wider, within the bound.
No kernel may reach another device: no remote copies, remote signals or barrier semaphores. Data moves between devices by JAX's collectives and lax.ppermute only.
A program may use at most 128 MiB of HBM per device.

v0:
```python
import jax
import jax.numpy as jnp
from jax import lax
from jax.sharding import PartitionSpec as P


def body(d_out, expert_ids, gate_weights, saved_gate, saved_up, w_gate, w_up, w_down, w_out):
    expert_count = lax.axis_size("expert")
    tp_count = lax.axis_size("tp")
    feat_local = d_out.shape[1]
    cap_slots = saved_gate.shape[1] // (expert_count * tp_count)
    model_width = w_gate.shape[1]
    experts_iota = jnp.arange(expert_count, dtype=jnp.int32)
    first_hit = expert_ids[:, 0:1] == experts_iota[None, :]
    second_hit = expert_ids[:, 1:2] == experts_iota[None, :]
    member = first_hit.astype(jnp.int32) + second_hit.astype(jnp.int32)
    weight = gate_weights[:, 0:1] * first_hit.astype(jnp.float32) + gate_weights[
        :, 1:2
    ] * second_hit.astype(jnp.float32)
    slot = jnp.cumsum(member, axis=0) - member
    slot_iota = jnp.arange(cap_slots, dtype=jnp.int32)
    select = ((slot[:, :, None] == slot_iota[None, None, :]) & (member[:, :, None] > 0)).astype(
        jnp.float32
    )
    weighted_sel = select * weight[:, :, None]
    outgoing = jnp.einsum(
        "tec,td->ecd", weighted_sel, d_out.astype(jnp.float32), precision=lax.Precision.HIGHEST
    ).astype(jnp.bfloat16)
    received = lax.all_to_all(outgoing, "expert", split_axis=0, concat_axis=0, tiled=True)
    blocks_all = lax.all_gather(received[:, None], "tp", axis=1, tiled=True)
    down_local = w_down[0]
    slot_rows = blocks_all.shape[0] * blocks_all.shape[1] * blocks_all.shape[2]
    shard_piece = lax.all_gather(blocks_all, "etp", axis=3, tiled=True)
    width_piece = shard_piece.shape[3]
    flat_rows = shard_piece.reshape(slot_rows, width_piece)
    grad_act = lax.dot_general(
        flat_rows, down_local, (((1,), (1,)), ((), ())), preferred_element_type=jnp.float32
    )
    gate_val = saved_gate[0].astype(jnp.float32)
    up_val = saved_up[0].astype(jnp.float32)
    sigma = jax.nn.sigmoid(gate_val)
    grad_up = (grad_act * gate_val * sigma).astype(jnp.bfloat16)
    grad_gate = (grad_act * up_val * sigma * (1.0 + gate_val * (1.0 - sigma))).astype(jnp.bfloat16)
    gate_local = w_gate[0]
    up_local = w_up[0]
    first_part = lax.dot_general(
        gate_local, grad_gate, (((1,), (1,)), ((), ())), preferred_element_type=jnp.float32
    )
    whole_term = (
        first_part
        + lax.dot_general(
            up_local, grad_up, (((1,), (1,)), ((), ())), preferred_element_type=jnp.float32
        )
    ).reshape(model_width, expert_count, tp_count, cap_slots)
    by_block = lax.psum_scatter(
        whole_term.astype(jnp.bfloat16), "tp", scatter_dimension=2, tiled=True
    )
    reduced = lax.psum_scatter(by_block, "etp", scatter_dimension=0, tiled=True).astype(jnp.float32)
    returned = lax.all_to_all(
        reduced.reshape(feat_local, expert_count, cap_slots).astype(jnp.bfloat16),
        "expert",
        split_axis=1,
        concat_axis=1,
        tiled=True,
    ).astype(jnp.float32)
    d_moe = jnp.einsum("tec,dec->td", select, returned, precision=lax.Precision.HIGHEST)
    d_hidden = (d_out.astype(jnp.float32) + d_moe).astype(jnp.bfloat16)
    head_partial = lax.dot_general(
        lax.all_gather(d_hidden, "tp", axis=0, tiled=True),
        w_out,
        (((1,), (1,)), ((), ())),
        preferred_element_type=jnp.float32,
    )
    d_heads = lax.psum_scatter(
        head_partial.astype(jnp.bfloat16), "etp", scatter_dimension=0, tiled=True
    )
    return (d_hidden, d_heads)


def solution(mesh):
    in_specs = (
        P(("expert", "tp"), "etp"),
        P(("expert", "tp"), None),
        P(("expert", "tp"), None),
        P("expert", None, ("etp", "tp")),
        P("expert", None, ("etp", "tp")),
        P("expert", None, ("etp", "tp")),
        P("expert", None, ("etp", "tp")),
        P("expert", ("etp", "tp"), None),
        P("tp", "etp"),
    )
    out_specs = (P(("expert", "tp"), "etp"), P(("expert", "etp"), "tp"))
    return jax.shard_map(body, mesh=mesh, in_specs=in_specs, out_specs=out_specs, check_vma=False)
```

profile of v0, /device:TPU:2, one launch (start us, length us, event | category | flops | bytes accessed | tf_op | source)
XLA Modules:
  0.0 581.8 jit_solution(4109981410665726276)
XLA Ops:
  7.2 0.8 slice_bitcast_fusion.3
  8.3 0.8 slice_bitcast_fusion.1
  9.1 0.2 select_add_fusion
  9.3 0.2 reduce_window_sum.11
  9.7 1.2 convolution_convert_fusion.1
  10.9 13.2 %all_to_all.10 = bf16[4,64,384]{2,1,0:T(8,128)(2,1)S(1)} all-to-all(bf16[4,64,384]{2,1,0:T(8,128)(2,1)S(1)} %convolution_convert_fusion.1), channel_id=1, replica_groups=mesh['expert'=4,'etp'=16,'tp'=4] {'expert'}, dimensions={0} | all-to-all | bytes 393216 | tf_op jit(solution)/shard_map/all_to_all | solution.py:29
  24.1 14.5 %all-gather = bf16[4,256,384]{2,1,0:T(8,128)(2,1)} all-gather(bf16[4,64,384]{2,1,0:T(8,128)(2,1)S(1)} %all_to_all.10), channel_id=2, replica_groups=mesh['expert'=4,'etp'=16,'tp'=4] {'tp'}, dimensions={1}, use_global_device_ids=true | all-gather | bytes 983040 | tf_op jit(solution)/shard_map/all_gather | solution.py:30
  38.7 103.7 %all-gather.3.cloned.1.call-done = bf16[4,4,64,6144]{3,2,1,0:T(8,128)(2,1)} async-done(((bf16[4,4,64,384]{3,2,1,0:T(8,128)(2,1)}), bf16[4,4,64,6144]{3,2,1,0:T(8,128)(2,1)}) %all-gather.3.cloned.1.call-update) | async-done | bytes 12582928 | tf_op jit(solution)/shard_map/all_gather | solution.py:33
  142.4 7.5 %fusion.3 = f32[1024,256]{1,0:T(8,128)S(1)} fusion(bf16[1024,6144]{1,0:T(8,128)(2,1)} %bitcast.60, bf16[1,256,6144]{2,1,0:T(8,128)(2,1)} %param.16), kind=kOutput, calls=%fused_computation.4 | convolution fusion | flops 3221225472 | bytes 16777216 | tf_op jit(solution)/shard_map/dot_general | solution.py:36
  149.9 1.0 copy-done.2
  150.9 10.4 %fusion.1 = f32[1024,6144]{1,0:T(8,128)} fusion(bf16[1,6144,256]{2,1,0:T(8,128)(2,1)S(1)} %copy-done, f32[1024,256]{1,0:T(8,128)S(1)} %fusion.3, bf16[1,1024,256]{2,1,0:T(8,128)(2,1)S(1)} %copy-done.4, bf16[1,1024,256]{2,1,0:T(8,128)(2,1)S(1)} %copy-done.3), kind=kOutput, calls=%fused_computation.2 | convolution fusion | flops 3224371200 | bytes 30408704 | tf_op jit(solution)/shard_map/dot_general | solution.py:46
  161.3 16.2 %add_convert_fusion = bf16[1024,6144]{1,0:T(8,128)(2,1)} fusion(f32[1024,6144]{1,0:T(8,128)} %fusion.1, bf16[1,6144,256]{2,1,0:T(8,128)(2,1)} %param.15, f32[1024,256]{1,0:T(8,128)} %copy-done.2, bf16[1,1024,256]{2,1,0:T(8,128)(2,1)} %param.12), kind=kOutput, calls=%fused_computation | convolution fusion | flops 3235643392 | bytes 42467328 | tf_op jit(solution)/shard_map/dot_general | solution.py:51
  177.5 10.9 %copy.18 = bf16[6144,4,4,64]{0,3,1,2:T(8,128)(2,1)} copy(bf16[6144,4,4,64]{0,3,2,1:T(8,128)(2,1)} %bitcast.55) | data formatting | bytes 25165824 | tf_op jit(solution)/shard_map/convert_element_type | solution.py:56
  188.5 183.0 %reduce-scatter.6.cloned.1.call-done = bf16[6144,4,1,64]{0,3,1,2:T(8,128)(2,1)} async-done(((bf16[6144,4,4,64]{0,3,1,2:T(8,128)(2,1)}), bf16[6144,4,1,64]{0,3,1,2:T(8,128)(2,1)}) %reduce-scatter.6.cloned.1.call-update) | async-done | bytes 3145744 | tf_op jit(solution)/shard_map/reduce_scatter | solution.py:55
  371.4 9.8 %copy.19 = bf16[6144,4,1,64]{3,1,2,0:T(4,128)(2,1)} copy(bf16[6144,4,1,64]{0,3,1,2:T(8,128)(2,1)} %reduce-scatter.6.cloned.1.call-done) | data formatting | bytes 6291456
  381.2 10.0 %reshape.232 = bf16[6144,256]{1,0:T(8,128)(2,1)} reshape(bf16[6144,1,4,64]{3,2,1,0:T(4,128)(2,1)} %bitcast.56) | data formatting | bytes 6291456
  391.3 77.7 %reduce-scatter.10.cloned.1.call-done = bf16[384,256]{1,0:T(8,128)(2,1)} async-done(((bf16[6144,256]{1,0:T(8,128)(2,1)}), bf16[384,256]{1,0:T(8,128)(2,1)}) %reduce-scatter.10.cloned.1.call-update) | async-done | bytes 196624
  469.0 1.2 reshape.233
  470.2 0.9 copy.20
  471.1 11.7 %all_to_all.11 = bf16[384,4,64]{0,2,1:T(8,128)(2,1)S(1)} all-to-all(bf16[384,4,64]{0,2,1:T(8,128)(2,1)} %bitcast.59), channel_id=1, replica_groups=mesh['expert'=4,'etp'=16,'tp'=4] {'expert'}, dimensions={1} | all-to-all | bytes 393216 | tf_op jit(solution)/shard_map/all_to_all | solution.py:59
  482.8 1.1 fusion.6
  483.9 10.0 %all_gather.11 = bf16[512,384]{1,0:T(8,128)(2,1)S(1)} all-gather(bf16[128,384]{1,0:T(8,128)(2,1)S(1)} %fusion.6), channel_id=1, replica_groups=mesh['expert'=4,'etp'=16,'tp'=4] {'tp'}, dimensions={0}, use_global_device_ids=true | all-gather | bytes 491520 | tf_op jit(solution)/shard_map/all_gather | solution.py:69
  494.0 3.4 convolution_convert_fusion
  497.4 77.8 %reduce-scatter.8.cloned.1.call-done = bf16[32,1536]{1,0:T(8,128)(2,1)} async-done(((bf16[512,1536]{1,0:T(8,128)(2,1)}), bf16[32,1536]{1,0:T(8,128)(2,1)}) %reduce-scatter.8.cloned.1.call-update) | async-done | bytes 98320 | tf_op jit(solution)/shard_map/reduce_scatter | solution.py:74
  (25 shorter events, 0.8 us)
Async XLA Ops:
  7.2 143.7 %copy-start = (bf16[1,6144,256]{2,1,0:T(8,128)(2,1)S(1)}, bf16[1,6144,256]{2,1,0:T(8,128)(2,1)}, u32[]{:S(2)}) copy-start(bf16[1,6144,256]{2,1,0:T(8,128)(2,1)} %param.14) | copy-start | bytes 9437188
  7.2 135.2 %all-gather.3.cloned.1.call-start = ((), (), s32[]{:S(2)}) async-start(), calls=%async_computation.5 | async-start | bytes 13369344 | tf_op jit(solution)/shard_map/all_gather | solution.py:33
  38.6 332.8 %reduce-scatter.6.cloned.1.call-start = ((), (), s32[]{:S(2)}) async-start(), calls=%async_computation.6 | async-start | bytes 15728640 | tf_op jit(solution)/shard_map/reduce_scatter | solution.py:55
  142.4 8.5 %copy-start.3 = (bf16[1,1024,256]{2,1,0:T(8,128)(2,1)S(1)}, bf16[1,1024,256]{2,1,0:T(8,128)(2,1)}, u32[]{:S(2)}) copy-start(bf16[1,1024,256]{2,1,0:T(8,128)(2,1)} %param.12) | copy-start | bytes 1572868
  142.4 8.5 %copy-start.4 = (bf16[1,1024,256]{2,1,0:T(8,128)(2,1)S(1)}, bf16[1,1024,256]{2,1,0:T(8,128)(2,1)}, u32[]{:S(2)}) copy-start(bf16[1,1024,256]{2,1,0:T(8,128)(2,1)} %param.13) | copy-start | bytes 1572868
  149.9 1.0 copy-start.2
  188.4 280.6 %reduce-scatter.10.cloned.1.call-start = ((), (), s32[]{:S(2)}) async-start(), calls=%async_computation.8 | async-start | bytes 3342336
  391.3 184.0 %reduce-scatter.8.cloned.1.call-start = ((), (), s32[]{:S(2)}) async-start(), calls=%async_computation.7 | async-start | bytes 1671168 | tf_op jit(solution)/shard_map/reduce_scatter | solution.py:74
  470.1 105.1 %copy-start.1 = (bf16[1,6144,256]{2,1,0:T(8,128)(2,1)S(1)}, bf16[1,6144,256]{2,1,0:T(8,128)(2,1)}, u32[]{:S(2)}) copy-start(bf16[1,6144,256]{2,1,0:T(8,128)(2,1)} %param.14) | copy-start | bytes 9437188
  483.9 91.3 %copy-start.5 = (bf16[128,384]{1,0:T(8,128)(2,1)}, bf16[128,384]{1,0:T(8,128)(2,1)S(1)}, u32[]{:S(2)}) copy-start(bf16[128,384]{1,0:T(8,128)(2,1)S(1)} %fusion.6) | copy-start | bytes 294916
Sparse Core Ops, SparseCore 0:
  38.8 103.5 all-gather.2
  188.5 182.8 reduce-scatter.5
  391.4 77.5 reduce-scatter.9
  497.6 77.6 reduce-scatter.7
where the time goes:
time: 583 us; the launch traced here: 582 us
  waiting for transfers between devices  442 us (76%)
  blocking collectives  49.4 us (8%)
  matrix products  39.9 us (7%)
  local copies, waits for them, and re-layouts  35.6 us (6%)
  between operations  13.9 us (2%)
    reduce_scatter x1, waiting for transfers between devices, body(): lax.psum_scatter(whole_term.astype(jnp.bfloat16), 'tp', scatter_dimension...  183 us
    all_gather x1, waiting for transfers between devices, body(): shard_piece = lax.all_gather(blocks_all, 'etp', axis=3, tiled=True)  104 us
    reduce_scatter x1, waiting for transfers between devices, body(): lax.psum_scatter(head_partial.astype(jnp.bfloat16), 'etp', scatter_dimens...  77.8 us
    unnamed x5, waiting for transfers between devices  77.7 us
    unnamed x16, local copies, waits for them, and re-layouts  22.9 us
    dot_general x1, matrix products, body(): lax.dot_general(up_local, grad_up, (((1,), (1,)), ((), ())), preferred_el...  16.2 us
    all_gather x1, blocking collectives, body(): blocks_all = lax.all_gather(received[:, None], 'tp', axis=1, tiled=True)  14.5 us
    all_to_all x1, blocking collectives, body(): lax.all_to_all(outgoing, 'expert', split_axis=0, concat_axis=0, tiled=True)  13.2 us
  transfers between devices with their start and end apart: 4, of which 4 were waited for; matrix products, arithmetic and copies ran while one was open for 0% of the time, Pallas kernels for 0%

commit v1 on v0

--- a/solution.py
+++ b/solution.py
@@ -30,7 +30,9 @@
     blocks_all = lax.all_gather(received[:, None], "tp", axis=1, tiled=True)
     down_local = w_down[0]
     slot_rows = blocks_all.shape[0] * blocks_all.shape[1] * blocks_all.shape[2]
-    shard_piece = lax.all_gather(blocks_all, "etp", axis=3, tiled=True)
+    shard_piece = jnp.concatenate(
+        lax.all_to_all(jnp.stack([blocks_all] * lax.axis_size("etp")), "etp", 0, 0), axis=3
+    )
     width_piece = shard_piece.shape[3]
     flat_rows = shard_piece.reshape(slot_rows, width_piece)
     grad_act = lax.dot_general(

time: 583 us -> 643 us (1.10)
  blocking collectives: 49.4 us -> 198 us
  waiting for transfers between devices: 442 us -> 335 us
  local copies, waits for them, and re-layouts: 35.6 us -> 56.1 us
    all_to_all x0 -> x1, blocking collectives: none -> 148 us  [body(): lax.all_to_all(jnp.stack([blocks_all] * lax.axis_size('etp')), 'etp', 0, 0)]
    all_gather x1 -> x0, waiting for transfers between devices: 104 us -> none  [body(): shard_piece = lax.all_gather(blocks_all, 'etp', axis=3, tiled=True)]
    reshape x0 -> x1, local copies, waits for them, and re-layouts: none -> 9.09 us  [body(): jnp.concatenate(lax.all_to_all(jnp.stack([blocks_all] * lax.axis_size('et...]
    another operation x0 -> x1, local copies, waits for them, and re-layouts: none -> 7.8 us  [body(): jnp.stack([blocks_all] * lax.axis_size('etp'))]
    unnamed x16 -> x17, local copies, waits for them, and re-layouts: 22.9 us -> 26.7 us
    unnamed x5 -> x4, waiting for transfers between devices: 77.7 us -> 77.6 us
  transfers between devices with their start and end apart: 4 -> 3, of which waited for: 4 -> 3; matrix products, arithmetic and copies ran while one was open for 0% -> 0% of each run, Pallas kernels for 0% -> 0%
where the time goes in v1:
time: 643 us; the launch traced here: 642 us
  waiting for transfers between devices  335 us (52%)
  blocking collectives  198 us (31%)
  local copies, waits for them, and re-layouts  56.1 us (9%)
  matrix products  37.7 us (6%)
  between operations  13.9 us (2%)
    reduce_scatter x1, waiting for transfers between devices, body(): lax.psum_scatter(whole_term.astype(jnp.bfloat16), 'tp', scatter_dimension...  180 us
    all_to_all x1, blocking collectives, body(): lax.all_to_all(jnp.stack([blocks_all] * lax.axis_size('etp')), 'etp', 0, 0)  148 us
    reduce_scatter x1, waiting for transfers between devices, body(): lax.psum_scatter(head_partial.astype(jnp.bfloat16), 'etp', scatter_dimens...  77.7 us
    unnamed x4, waiting for transfers between devices  77.6 us
    unnamed x17, local copies, waits for them, and re-layouts  26.7 us
    dot_general x1, matrix products, body(): lax.dot_general(up_local, grad_up, (((1,), (1,)), ((), ())), preferred_el...  16.2 us
    all_gather x1, blocking collectives, body(): blocks_all = lax.all_gather(received[:, None], 'tp', axis=1, tiled=True)  14.5 us
    all_to_all x1, blocking collectives, body(): lax.all_to_all(outgoing, 'expert', split_axis=0, concat_axis=0, tiled=True)  13.2 us
  transfers between devices with their start and end apart: 3, of which 3 were waited for; matrix products, arithmetic and copies ran while one was open for 0% of the time, Pallas kernels for 0%

profile of v1, /device:TPU:2, one launch (start us, length us, event | category | flops | bytes accessed | tf_op | source)
XLA Modules:
  0.0 641.9 jit_solution(16197531364429572122)
XLA Ops:
  7.2 0.8 slice_bitcast_fusion.3
  9.7 1.2 convolution_convert_fusion.1
  10.9 13.2 %all_to_all.15 = bf16[4,64,384]{2,1,0:T(8,128)(2,1)S(1)} all-to-all(bf16[4,64,384]{2,1,0:T(8,128)(2,1)S(1)} %convolution_convert_fusion.1), channel_id=1, replica_groups=mesh['expert'=4,'etp'=16,'tp'=4] {'expert'}, dimensions={0} | all-to-all | bytes 393216 | tf_op jit(solution)/shard_map/all_to_all | solution.py:29
  24.1 14.5 %all-gather = bf16[4,256,384]{2,1,0:T(8,128)(2,1)} all-gather(bf16[4,64,384]{2,1,0:T(8,128)(2,1)S(1)} %all_to_all.15), channel_id=2, replica_groups=mesh['expert'=4,'etp'=16,'tp'=4] {'tp'}, dimensions={1}, use_global_device_ids=true | all-gather | bytes 983040 | tf_op jit(solution)/shard_map/all_gather | solution.py:30
  38.6 7.8 %stack.2 = bf16[16,4,4,64,384]{4,3,2,1,0:T(8,128)(2,1)} broadcast(bf16[4,4,64,384]{3,2,1,0:T(8,128)(2,1)} %bitcast.63), dimensions={1,2,3,4} | broadcast | bytes 13369344 | tf_op jit(solution)/shard_map/stack | solution.py:34
  46.4 148.4 %all_to_all.16 = bf16[16,4,4,64,384]{4,3,2,1,0:T(8,128)(2,1)S(1)} all-to-all(bf16[16,4,4,64,384]{4,3,2,1,0:T(8,128)(2,1)} %stack.2), channel_id=1, replica_groups=mesh['expert'=4,'etp'=16,'tp'=4] {'etp'}, dimensions={0} | all-to-all | bytes 25165824 | tf_op jit(solution)/shard_map/all_to_all | solution.py:34
  194.8 9.1 %copy.22 = bf16[4,4,64,16,384]{4,3,2,1,0:T(8,128)(2,1)S(1)} copy(bf16[4,4,64,16,384]{4,2,1,0,3:T(8,128)(2,1)S(1)} %bitcast.59) | data formatting | bytes 25165824 | tf_op jit(solution)/shard_map/reshape | solution.py:33
  203.9 3.8 copy.26
  207.7 5.4 fusion.3
  213.2 1.0 copy-done.2
  214.1 10.3 %fusion.1 = f32[1024,6144]{1,0:T(8,128)} fusion(bf16[1,6144,256]{2,1,0:T(8,128)(2,1)S(1)} %copy-done, f32[1024,256]{1,0:T(8,128)S(1)} %fusion.3, bf16[1,1024,256]{2,1,0:T(8,128)(2,1)S(1)} %copy-done.4, bf16[1,1024,256]{2,1,0:T(8,128)(2,1)S(1)} %copy-done.3), kind=kOutput, calls=%fused_computation.2 | convolution fusion | flops 3224371200 | bytes 30408704 | tf_op jit(solution)/shard_map/dot_general | solution.py:48
  224.4 16.2 %add_convert_fusion = bf16[1024,6144]{1,0:T(8,128)(2,1)} fusion(f32[1024,6144]{1,0:T(8,128)} %fusion.1, bf16[1,6144,256]{2,1,0:T(8,128)(2,1)} %param.15, f32[1024,256]{1,0:T(8,128)} %copy-done.2, bf16[1,1024,256]{2,1,0:T(8,128)(2,1)} %param.12), kind=kOutput, calls=%fused_computation | convolution fusion | flops 3235643392 | bytes 42467328 | tf_op jit(solution)/shard_map/dot_general | solution.py:53
  240.7 10.7 %copy.23 = bf16[6144,4,4,64]{0,3,1,2:T(8,128)(2,1)} copy(bf16[6144,4,4,64]{0,3,2,1:T(8,128)(2,1)} %bitcast.58) | data formatting | bytes 25165824 | tf_op jit(solution)/shard_map/convert_element_type | solution.py:58
  251.6 180.2 %reduce-scatter.6.cloned.1.call-done = bf16[6144,4,1,64]{0,3,1,2:T(8,128)(2,1)} async-done(((bf16[6144,4,4,64]{0,3,1,2:T(8,128)(2,1)}), bf16[6144,4,1,64]{0,3,1,2:T(8,128)(2,1)}) %reduce-scatter.6.cloned.1.call-update) | async-done | bytes 3145744 | tf_op jit(solution)/shard_map/reduce_scatter | solution.py:57
  431.8 9.8 %copy.24 = bf16[6144,4,1,64]{3,1,2,0:T(4,128)(2,1)} copy(bf16[6144,4,1,64]{0,3,1,2:T(8,128)(2,1)} %reduce-scatter.6.cloned.1.call-done) | data formatting | bytes 6291456
  441.6 10.0 %reshape.234 = bf16[6144,256]{1,0:T(8,128)(2,1)} reshape(bf16[6144,1,4,64]{3,2,1,0:T(4,128)(2,1)} %bitcast.61) | data formatting | bytes 6291456
  451.7 77.5 %reduce-scatter.10.cloned.1.call-done = bf16[384,256]{1,0:T(8,128)(2,1)} async-done(((bf16[6144,256]{1,0:T(8,128)(2,1)}), bf16[384,256]{1,0:T(8,128)(2,1)}) %reduce-scatter.10.cloned.1.call-update) | async-done | bytes 196624
  529.2 1.2 reshape.235
  530.4 0.9 copy.25
  531.3 11.7 %all_to_all.17 = bf16[384,4,64]{0,2,1:T(8,128)(2,1)S(1)} all-to-all(bf16[384,4,64]{0,2,1:T(8,128)(2,1)} %bitcast.65), channel_id=1, replica_groups=mesh['expert'=4,'etp'=16,'tp'=4] {'expert'}, dimensions={1} | all-to-all | bytes 393216 | tf_op jit(solution)/shard_map/all_to_all | solution.py:61
  543.1 1.1 fusion.6
  544.2 10.0 %all_gather.7 = bf16[512,384]{1,0:T(8,128)(2,1)S(1)} all-gather(bf16[128,384]{1,0:T(8,128)(2,1)S(1)} %fusion.6), channel_id=1, replica_groups=mesh['expert'=4,'etp'=16,'tp'=4] {'tp'}, dimensions={0}, use_global_device_ids=true | all-gather | bytes 491520 | tf_op jit(solution)/shard_map/all_gather | solution.py:71
  554.2 3.4 convolution_convert_fusion
  557.7 77.7 %reduce-scatter.8.cloned.1.call-done = bf16[32,1536]{1,0:T(8,128)(2,1)} async-done(((bf16[512,1536]{1,0:T(8,128)(2,1)}), bf16[32,1536]{1,0:T(8,128)(2,1)}) %reduce-scatter.8.cloned.1.call-update) | async-done | bytes 98320 | tf_op jit(solution)/shard_map/reduce_scatter | solution.py:76
  (26 shorter events, 2.0 us)
Async XLA Ops:
  7.2 207.0 %copy-start = (bf16[1,6144,256]{2,1,0:T(8,128)(2,1)S(1)}, bf16[1,6144,256]{2,1,0:T(8,128)(2,1)}, u32[]{:S(2)}) copy-start(bf16[1,6144,256]{2,1,0:T(8,128)(2,1)} %param.14) | copy-start | bytes 9437188
  7.2 424.7 %reduce-scatter.6.cloned.1.call-start = ((), (), s32[]{:S(2)}) async-start(), calls=%async_computation.6 | async-start | bytes 15728640 | tf_op jit(solution)/shard_map/reduce_scatter | solution.py:57
  207.7 6.4 %copy-start.3 = (bf16[1,1024,256]{2,1,0:T(8,128)(2,1)S(1)}, bf16[1,1024,256]{2,1,0:T(8,128)(2,1)}, u32[]{:S(2)}) copy-start(bf16[1,1024,256]{2,1,0:T(8,128)(2,1)} %param.12) | copy-start | bytes 1572868
  207.7 6.4 %copy-start.4 = (bf16[1,1024,256]{2,1,0:T(8,128)(2,1)S(1)}, bf16[1,1024,256]{2,1,0:T(8,128)(2,1)}, u32[]{:S(2)}) copy-start(bf16[1,1024,256]{2,1,0:T(8,128)(2,1)} %param.13) | copy-start | bytes 1572868
  213.2 1.0 copy-start.2
  251.4 277.8 %reduce-scatter.10.cloned.1.call-start = ((), (), s32[]{:S(2)}) async-start(), calls=%async_computation.8 | async-start | bytes 3342336
  451.7 183.7 %reduce-scatter.8.cloned.1.call-start = ((), (), s32[]{:S(2)}) async-start(), calls=%async_computation.7 | async-start | bytes 1671168 | tf_op jit(solution)/shard_map/reduce_scatter | solution.py:76
  530.4 105.0 %copy-start.1 = (bf16[1,6144,256]{2,1,0:T(8,128)(2,1)S(1)}, bf16[1,6144,256]{2,1,0:T(8,128)(2,1)}, u32[]{:S(2)}) copy-start(bf16[1,6144,256]{2,1,0:T(8,128)(2,1)} %param.14) | copy-start | bytes 9437188
  544.2 91.2 %copy-start.5 = (bf16[128,384]{1,0:T(8,128)(2,1)}, bf16[128,384]{1,0:T(8,128)(2,1)S(1)}, u32[]{:S(2)}) copy-start(bf16[128,384]{1,0:T(8,128)(2,1)S(1)} %fusion.6) | copy-start | bytes 294916
Sparse Core Ops, SparseCore 0:
  251.5 180.2 reduce-scatter.5
  451.8 77.3 reduce-scatter.9
  557.8 77.5 reduce-scatter.7
